TPU v7x, 32 devices: a whole 2x2x4 slice. The times are simulated.
32 devices in a mesh: group: 2 (over x), tensor: 8 (over z, y), dp: 2 (over core).
Axes of the slice: x: 2, y: 2, z: 4, core: 2. Of those that a mesh axis runs over, the one named last changes fastest.
Arguments:
- features: bfloat16 [512, 8192], P(('group', 'dp'), 'tensor'), parts along dimension 0, may hold values from -64 to 64
- cotangent: bfloat16 [512, 8192], P(('group', 'dp'), 'tensor'), parts along dimension 0, may hold values from -64 to 64
- token_tenant: int32 [512], P(('group', 'dp')), parts along dimension 0, may hold values from 0 to 15
- owner_device: int32 [32], P('group'), parts along dimension 0, may hold values from 0 to 15, each once
- frozen_weight: bfloat16 [8192, 8192], P('tensor'), may hold values from -0.09375 to 0.09375
- adapter_down: bfloat16 [32, 16, 8192], P('group', None, 'tensor'), parts along dimension 0, may hold values from -0.0625 to 0.0625
- adapter_up: bfloat16 [32, 16, 8192], P('group', None, 'tensor'), parts along dimension 0, may hold values from -0.29882812 to 0.29882812
- momentum_down: float32 [32, 16, 8192], P(('group', 'tensor', 'dp')), parts along dimension 0, may hold values from -12 to 12
- momentum_up: float32 [32, 16, 8192], P(('group', 'tensor', 'dp')), parts along dimension 0, may hold values from -3 to 3
- variance_down: float32 [32, 16, 8192], P(('group', 'tensor', 'dp')), parts along dimension 0, may hold values from 0.3 to 3
- variance_up: float32 [32, 16, 8192], P(('group', 'tensor', 'dp')), parts along dimension 0, may hold values from 0.02 to 0.2
Outputs:
- projected: bfloat16 [512, 8192], P(('group', 'dp'), 'tensor'), parts along dimension 0
- updated_down: bfloat16 [32, 16, 8192], P('group', None, 'tensor'), parts along dimension 0
- updated_up: bfloat16 [32, 16, 8192], P('group', None, 'tensor'), parts along dimension 0
- mean_down: float32 [32, 16, 8192], P(('group', 'tensor', 'dp')), parts along dimension 0
- mean_up: float32 [32, 16, 8192], P(('group', 'tensor', 'dp')), parts along dimension 0
- power_down: float32 [32, 16, 8192], P(('group', 'tensor', 'dp')), parts along dimension 0
- power_up: float32 [32, 16, 8192], P(('group', 'tensor', 'dp')), parts along dimension 0
There are 2 independent parts, one for each index of `group`. A program takes and returns all parts, laid end to end along the dimension named above; an argument that names none is the same for every part. Nothing has to cross between parts.
Inputs may be any that keep to these rules, and one draw needn't show every extreme that they name: Tenant t belongs to the device whose index along tensor+dp (dp fastest) is owner_device[t]; every index appears once.
All inputs are finite; a program needn't handle non-finite values.
Results may differ from a plain program's by a relative error of at most 0.0014.
The roundings to bfloat16 on the way count: a program that leaves them out, or rounds other values in their place, can miss the bound.
Values sent between devices are 32-bit elements; how exact they have to be, the bound alone decides.
A program may use at most 128 MiB of HBM per device.

v0:
```python
import jax
import jax.numpy as jnp
from jax import lax
from jax.sharding import PartitionSpec as P

adapter_scale = 2.0
clip_norm = 12000.0
learn_rate = 0.004
beta_one = 0.9
beta_two = 0.999
adam_eps = 1e-08
correct_one = 1.0 - beta_one**20
correct_two = 1.0 - beta_two**20


def tenant_mask(token_tenant, tenants, lowrank):
    columns = lax.broadcasted_iota(jnp.int32, (1, tenants * lowrank), 1) // lowrank
    return token_tenant[:, None] == columns


def rank_fold(tenants, lowrank):
    row_index = lax.broadcasted_iota(jnp.int32, (tenants * lowrank, lowrank), 0) % lowrank
    col_index = lax.broadcasted_iota(jnp.int32, (tenants * lowrank, lowrank), 1)
    return (row_index == col_index).astype(jnp.float32)


def select_rank(scores, token_mask, folding):
    picked = jnp.where(token_mask, scores, jnp.zeros_like(scores))
    return jnp.dot(
        picked, folding, precision=lax.Precision.HIGHEST, preferred_element_type=jnp.float32
    )


def spread_rank(values, token_mask, tenants):
    scaled = (adapter_scale * values).astype(jnp.bfloat16)
    tiled_rank = jnp.tile(scaled, (1, tenants))
    return jnp.where(token_mask, tiled_rank, jnp.zeros_like(tiled_rank))


def owner_order(owner_device):
    total = owner_device.shape[0]
    slot_index = lax.broadcasted_iota(jnp.int32, (total, total), 0)
    tenant_index = lax.broadcasted_iota(jnp.int32, (total, total), 1)
    return jnp.sum(jnp.where(owner_device[None, :] == slot_index, tenant_index, 0), axis=1)


def adam_step(gradient, factor, moment, square):
    clipped = gradient * factor
    moment_next = beta_one * moment + (1.0 - beta_one) * clipped
    square_next = beta_two * square + (1.0 - beta_two) * clipped * clipped
    change = (
        learn_rate * (moment_next / correct_one) / (jnp.sqrt(square_next / correct_two) + adam_eps)
    )
    return (moment_next, square_next, change)


def frozen_blocks(features, frozen_weight, width_shard, blocks):
    columns = frozen_weight
    columns = columns.reshape(frozen_weight.shape[0], blocks, width_shard)
    return jnp.einsum("ti,ibc->btc", features, columns, preferred_element_type=jnp.float32)


def on_device(
    features,
    cotangent,
    token_tenant,
    owner_device,
    frozen_weight,
    adapter_down,
    adapter_up,
    momentum_down,
    momentum_up,
    variance_down,
    variance_up,
):
    tokens = features.shape[0]
    tenants, lowrank, width_shard = adapter_down.shape
    parts_tensor = lax.axis_size("tensor")
    parts_dp = lax.axis_size("dp")
    token_mask = tenant_mask(token_tenant, tenants, lowrank)
    folding = rank_fold(tenants, lowrank)
    down_flat = adapter_down.reshape(tenants * lowrank, width_shard)
    up_flattened = adapter_up.reshape(tenants * lowrank, width_shard)
    contract = (((1,), (1,)), ((), ()))
    down_part = select_rank(
        lax.dot_general(features, down_flat, contract, preferred_element_type=jnp.float32),
        token_mask,
        folding,
    )
    up_part = select_rank(
        lax.dot_general(cotangent, up_flattened, contract, preferred_element_type=jnp.float32),
        token_mask,
        folding,
    )
    blocks = lax.axis_size("tensor") * tokens // tokens
    result = frozen_blocks(features, frozen_weight, width_shard, blocks)
    frozen_result = lax.psum_scatter(
        result.reshape(blocks * tokens, width_shard), "tensor", scatter_dimension=0, tiled=True
    )
    down_sum, up_sum = lax.psum((down_part, up_part), "tensor")
    down_scattered = spread_rank(down_sum, token_mask, tenants)
    up_scattered = spread_rank(up_sum, token_mask, tenants)
    adapter_result = jnp.dot(down_scattered, up_flattened, preferred_element_type=jnp.float32)
    projected = (frozen_result + adapter_result).astype(jnp.bfloat16)
    outer_product = (((0,), (0,)), ((), ()))
    down_gradient = lax.dot_general(
        up_scattered, features, outer_product, preferred_element_type=jnp.float32
    )
    up_gradient = lax.dot_general(
        down_scattered, cotangent, outer_product, preferred_element_type=jnp.float32
    )
    down_gradient = down_gradient.reshape(tenants, lowrank, width_shard)
    up_gradient = up_gradient.reshape(tenants, lowrank, width_shard)
    slot_tenant = owner_order(owner_device)
    half_index = lax.broadcasted_iota(jnp.int32, (tenants,), 0)
    slot_index = half_index % parts_tensor * parts_dp + half_index // parts_tensor
    half_tenant = jnp.take(slot_tenant, slot_index, axis=0)
    down_halves = jnp.take(down_gradient, half_tenant, axis=0)
    up_halves = jnp.take(up_gradient, half_tenant, axis=0)
    summed = (
        lax.psum_scatter(down_halves, "dp", scatter_dimension=0, tiled=True),
        lax.psum_scatter(up_halves, "dp", scatter_dimension=0, tiled=True),
    )
    own_down, own_up = (
        lax.all_to_all(summed[0], "tensor", split_axis=0, concat_axis=2, tiled=True),
        lax.all_to_all(summed[1], "tensor", split_axis=0, concat_axis=2, tiled=True),
    )
    squares = jnp.sum(own_down * own_down) + jnp.sum(own_up * own_up)
    factor = clip_norm / jnp.maximum(jnp.sqrt(squares), clip_norm)
    mean_down, power_down, change_down = adam_step(own_down, factor, momentum_down, variance_down)
    mean_up, power_up, change_up = adam_step(own_up, factor, momentum_up, variance_up)
    pieces = (
        lax.all_to_all(change_down, ("tensor", "dp"), split_axis=2, concat_axis=0, tiled=True),
        lax.all_to_all(change_up, ("tensor", "dp"), split_axis=2, concat_axis=0, tiled=True),
    )
    joined = (
        lax.all_gather(pieces[0], "dp", axis=2, tiled=True),
        lax.all_gather(pieces[1], "dp", axis=2, tiled=True),
    )
    back_down = jnp.take(joined[0], owner_device, axis=0)
    back_up = jnp.take(joined[1], owner_device, axis=0)
    updated_down = (adapter_down.astype(jnp.float32) - back_down).astype(jnp.bfloat16)
    updated_up = (adapter_up.astype(jnp.float32) - back_up).astype(jnp.bfloat16)
    return (projected, updated_down, updated_up, mean_down, mean_up, power_down, power_up)


def solution(mesh):
    in_specs = (
        P(("group", "dp"), "tensor"),
        P(("group", "dp"), "tensor"),
        P(("group", "dp")),
        P("group"),
        P("tensor", None),
        P("group", None, "tensor"),
        P("group", None, "tensor"),
        P(("group", "tensor", "dp"), None, None),
        P(("group", "tensor", "dp"), None, None),
        P(("group", "tensor", "dp"), None, None),
        P(("group", "tensor", "dp"), None, None),
    )
    out_specs = (
        P(("group", "dp"), "tensor"),
        P("group", None, "tensor"),
        P("group", None, "tensor"),
        P(("group", "tensor", "dp"), None, None),
        P(("group", "tensor", "dp"), None, None),
        P(("group", "tensor", "dp"), None, None),
        P(("group", "tensor", "dp"), None, None),
    )
    return jax.shard_map(
        on_device, mesh=mesh, in_specs=in_specs, out_specs=out_specs, check_vma=False
    )
```

profile of v0, /device:TPU:0, one launch (start us, length us, event | category | flops | bytes accessed | tf_op | source)
XLA Modules:
  0.0 376.7 jit_solution(10851005240872450794)
XLA Ops:
  8.1 1.5 convolution_select_fusion
  9.6 1.4 convolution_select_fusion.1
  11.8 38.9 %all-reduce = (f32[128,16]{0,1:T(8,128)S(1)}, f32[128,16]{0,1:T(8,128)S(1)}) all-reduce(f32[128,16]{0,1:T(8,128)S(1)} %fusion.15, f32[128,16]{0,1:T(8,128)S(1)} %fusion.14), channel_id=1, replica_groups=mesh['group'=2,'tensor'=8,'dp'=2] {'tensor'}, use_global_device_ids=true, to_apply=%region_1.2 | all-reduce | flops 4096 | bytes 32768 | tf_op jit(solution)/shard_map/psum | solution.py:100
  54.6 1.6 broadcast_select_fusion
  57.0 5.0 %reduce-scatter.8.cloned.1.call-done = f32[8,16,1024]{2,1,0:T(8,128)} async-done(((f32[16,16,1024]{2,1,0:T(8,128)}), f32[8,16,1024]{2,1,0:T(8,128)}) %reduce-scatter.8.cloned.1.call-update) | async-done | bytes 524304 | tf_op jit(solution)/shard_map/reduce_scatter | solution.py:122
  62.0 5.8 %all-to-all-start.1 = ((f32[8,16,1024]{2,1,0:T(8,128)}), f32[8,16,1024]{2,1,0:T(8,128)S(1)}, u32[]{:S(2)}, u32[]{:S(2)}) async-start(f32[8,16,1024]{2,1,0:T(8,128)} %reduce-scatter.8.cloned.1.call-done), calls=%async_computation.4 | async-start | bytes 1048576 | tf_op jit(solution)/shard_map/all_to_all | solution.py:126
  67.8 6.0 %reduce-scatter.6.cloned.1.call-done = f32[8,16,1024]{2,1,0:T(8,128)} async-done(((f32[16,16,1024]{2,1,0:T(8,128)}), f32[8,16,1024]{2,1,0:T(8,128)}) %reduce-scatter.6.cloned.1.call-update) | async-done | bytes 524304 | tf_op jit(solution)/shard_map/reduce_scatter | solution.py:121
  73.9 8.9 %all-to-all-done.1 = f32[8,16,1024]{2,1,0:T(8,128)S(1)} async-done(((f32[8,16,1024]{2,1,0:T(8,128)}), f32[8,16,1024]{2,1,0:T(8,128)S(1)}, u32[]{:S(2)}, u32[]{:S(2)}) %all-to-all-start.1) | async-done | bytes 524320 | tf_op jit(solution)/shard_map/all_to_all | solution.py:126
  82.7 3.6 all-to-all-start
  87.1 13.9 %all-to-all-done = f32[8,16,1024]{2,1,0:T(8,128)S(1)} async-done(((f32[8,16,1024]{2,1,0:T(8,128)}), f32[8,16,1024]{2,1,0:T(8,128)S(1)}, u32[]{:S(2)}, u32[]{:S(2)}) %all-to-all-start) | async-done | bytes 524320 | tf_op jit(solution)/shard_map/all_to_all | solution.py:125
  103.3 1.3 add_divide_fusion.1
  104.5 6.4 %copy.46 = f32[1,16,8192]{1,0,2:T(1,128)} copy(f32[1,16,8192]{2,1,0:T(8,128)S(1)} %get-tuple-element.13) | data formatting | bytes 1048576 | tf_op jit(solution)/shard_map/div | solution.py:52
  111.5 38.4 %reduce.8 = f32[8192,16]{1,0:T(8,128)} reduce(f32[8192,1,16]{2,1,0:T(1,128)} %bitcast.66, f32[]{:T(128)} %broadcast.462), dimensions={1}, to_apply=%bitcast.51.reduce_sub_computation | reduce | bytes 1048580
  149.9 4.2 %reshape.313 = f32[16,1,8192]{2,1,0:T(1,128)} reshape(f32[8192,16]{1,0:T(8,128)} %reduce.8) | data formatting | bytes 1048576
  154.1 3.7 all-to-all-start.2
  158.2 13.9 %all-to-all-done.2 = f32[16,1,8192]{2,1,0:T(1,128)S(1)} async-done(((f32[16,1,8192]{2,1,0:T(1,128)}), f32[16,1,8192]{2,1,0:T(1,128)S(1)}, u32[]{:S(2)}, u32[]{:S(2)}) %all-to-all-start.2) | async-done | bytes 524320 | tf_op jit(solution)/shard_map/all_to_all | solution.py:133
  172.1 1.9 reduce.9
  174.0 9.3 %reshape.314 = f32[8192,1,16]{2,1,0:T(1,128)} reshape(f32[16,8192]{1,0:T(8,128)S(1)} %reduce.9) | data formatting | bytes 1048576
  183.3 3.5 copy.48
  188.2 6.4 %copy.50 = f32[1,16,8192]{1,0,2:T(1,128)} copy(f32[1,16,8192]{2,1,0:T(8,128)S(1)} %get-tuple-element.10) | data formatting | bytes 1048576 | tf_op jit(solution)/shard_map/div | solution.py:52
  194.6 38.4 %reduce.6 = f32[8192,16]{1,0:T(8,128)} reduce(f32[8192,1,16]{2,1,0:T(1,128)} %bitcast.67, f32[]{:T(128)} %broadcast.462), dimensions={1}, to_apply=%bitcast.53.reduce_sub_computation | reduce | bytes 1048580
  233.0 3.5 reshape.315
  236.5 18.4 %all_to_all.54 = f32[16,1,8192]{2,1,0:T(1,128)S(1)} all-to-all(f32[16,1,8192]{2,1,0:T(1,128)S(1)} %reshape.315), channel_id=1, replica_groups=mesh['group'=2,'tensor'=8,'dp'=2] {'tensor','dp'}, dimensions={0} | all-to-all | bytes 1048576 | tf_op jit(solution)/shard_map/all_to_all | solution.py:134
  254.9 1.9 reduce.7
  256.8 9.3 %reshape.316 = f32[8192,1,16]{2,1,0:T(1,128)} reshape(f32[16,8192]{1,0:T(8,128)S(1)} %reduce.7) | data formatting | bytes 1048576
  266.0 3.5 copy.52
  269.6 10.1 %fusion = f32[8,1024,128]{1,2,0:T(8,128)} fusion(bf16[128,8,8,1024]{3,2,1,0:T(8,128)(2,1)} %bitcast.81, bf16[128,1024]{1,0:T(8,128)(2,1)S(1)} %copy-done), kind=kOutput, calls=%fused_computation.5 | convolution fusion | flops 2147483648 | bytes 21233664 | tf_op jit(solution)/shard_map/ti,ibc->btc/dot_general | solution.py:60
  279.9 1.9 gather_fusion.3
  281.8 1.8 gather_fusion.4
  283.7 1.4 fusion.5
  285.1 82.4 %reduce-scatter.4.cloned.1.call-done = f32[128,1024]{1,0:T(8,128)} async-done(((f32[1024,1024]{1,0:T(8,128)}), f32[128,1024]{1,0:T(8,128)}) %reduce-scatter.4.cloned.1.call-update) | async-done | bytes 524304 | tf_op jit(solution)/shard_map/reduce_scatter | solution.py:97
  367.5 2.1 fusion.4
  (68 shorter events, 9.3 us)
Async XLA Ops:
  8.0 1.6 copy-start
  8.0 45.0 %copy-start.3 = (bf16[128,1024]{1,0:T(8,128)(2,1)S(1)}, bf16[128,1024]{1,0:T(8,128)(2,1)}, u32[]{:S(2)}) copy-start(bf16[128,1024]{1,0:T(8,128)(2,1)} %param.14) | copy-start | bytes 786436
  8.0 44.1 %copy-start.9 = (s32[16]{0:T(128)S(1)}, s32[16]{0:T(128)}, u32[]{:S(2)}) copy-start(s32[16]{0:T(128)} %param.16) | copy-start | bytes 196
  8.0 54.0 %reduce-scatter.8.cloned.1.call-start = ((), (), s32[]{:S(2)}) async-start(), calls=%async_computation.9 | async-start | bytes 1572864 | tf_op jit(solution)/shard_map/reduce_scatter | solution.py:122
  56.2 47.1 %copy-start.4 = (f32[1,16,8192]{2,1,0:T(8,128)S(1)}, f32[1,16,8192]{2,1,0:T(8,128)}, u32[]{:S(2)}) copy-start(f32[1,16,8192]{2,1,0:T(8,128)} %param.20) | copy-start | bytes 1572868
  56.2 47.1 %copy-start.5 = (f32[1,16,8192]{2,1,0:T(8,128)S(1)}, f32[1,16,8192]{2,1,0:T(8,128)}, u32[]{:S(2)}) copy-start(f32[1,16,8192]{2,1,0:T(8,128)} %param.22) | copy-start | bytes 1572868
  56.2 17.7 %reduce-scatter.6.cloned.1.call-start = ((), (), s32[]{:S(2)}) async-start(), calls=%async_computation.8 | async-start | bytes 1572864 | tf_op jit(solution)/shard_map/reduce_scatter | solution.py:121
  62.0 20.7 %all-to-all-start.1 = ((f32[8,16,1024]{2,1,0:T(8,128)}), f32[8,16,1024]{2,1,0:T(8,128)S(1)}, u32[]{:S(2)}, u32[]{:S(2)}) async-start(f32[8,16,1024]{2,1,0:T(8,128)} %reduce-scatter.8.cloned.1.call-done), calls=%async_computation.4 | async-start | bytes 1048576 | tf_op jit(solution)/shard_map/all_to_all | solution.py:126
  82.7 18.3 %all-to-all-start = ((f32[8,16,1024]{2,1,0:T(8,128)}), f32[8,16,1024]{2,1,0:T(8,128)S(1)}, u32[]{:S(2)}, u32[]{:S(2)}) async-start(f32[8,16,1024]{2,1,0:T(8,128)} %reduce-scatter.6.cloned.1.call-done), calls=%async_computation.2 | async-start | bytes 1048576 | tf_op jit(solution)/shard_map/all_to_all | solution.py:125
  154.1 18.0 %all-to-all-start.2 = ((f32[16,1,8192]{2,1,0:T(1,128)}), f32[16,1,8192]{2,1,0:T(1,128)S(1)}, u32[]{:S(2)}, u32[]{:S(2)}) async-start(f32[16,1,8192]{2,1,0:T(1,128)} %reshape.313), calls=%async_computation.5 | async-start | bytes 1048576 | tf_op jit(solution)/shard_map/all_to_all | solution.py:133
  157.8 122.0 %all-gather.5.cloned.1.call-start = ((), (), s32[]{:S(2)}) async-start(), calls=%async_computation.10 | async-start | bytes 1572864 | tf_op jit(solution)/shard_map/all_gather | solution.py:137
  174.0 12.9 %copy-start.6 = (f32[1,16,8192]{2,1,0:T(8,128)S(1)}, f32[1,16,8192]{2,1,0:T(8,128)}, u32[]{:S(2)}) copy-start(f32[1,16,8192]{2,1,0:T(8,128)} %param.21) | copy-start | bytes 1572868
  174.0 12.9 %copy-start.7 = (f32[1,16,8192]{2,1,0:T(8,128)S(1)}, f32[1,16,8192]{2,1,0:T(8,128)}, u32[]{:S(2)}) copy-start(f32[1,16,8192]{2,1,0:T(8,128)} %param.23) | copy-start | bytes 1572868
  186.8 95.0 %all-gather.7.cloned.1.call-start = ((), (), s32[]{:S(2)}) async-start(), calls=%async_computation.11 | async-start | bytes 1572864 | tf_op jit(solution)/shard_map/all_gather | solution.py:138
  269.6 97.9 %reduce-scatter.4.cloned.1.call-start = ((), (), s32[]{:S(2)}) async-start(), calls=%async_computation.7 | async-start | bytes 4718592 | tf_op jit(solution)/shard_map/reduce_scatter | solution.py:97
  279.7 3.9 %copy-start.1 = (bf16[16,16,1024]{2,1,0:T(8,128)(2,1)S(1)}, bf16[16,16,1024]{2,1,0:T(8,128)(2,1)}, u32[]{:S(2)}) copy-start(bf16[16,16,1024]{2,1,0:T(8,128)(2,1)} %param.19) | copy-start | bytes 1572868
  279.7 3.9 %copy-start.2 = (bf16[16,16,1024]{2,1,0:T(8,128)(2,1)S(1)}, bf16[16,16,1024]{2,1,0:T(8,128)(2,1)}, u32[]{:S(2)}) copy-start(bf16[16,16,1024]{2,1,0:T(8,128)(2,1)} %param.18) | copy-start | bytes 1572868
  279.9 87.6 %copy-start.8 = (s32[128]{0:T(128)S(1)}, s32[128]{0:T(128)}, u32[]{:S(2)}) copy-start(s32[128]{0:T(128)} %param.15) | copy-start | bytes 1540
Sparse Core Ops, SparseCore 0:
  56.3 5.6 reduce-scatter.7
  64.2 9.5 reduce-scatter.5
  186.9 8.5 all-gather.4
  269.7 8.5 all-gather.6
Sparse Core Ops, SparseCore 1:
  279.9 87.5 reduce-scatter.3
where the time goes:
time: 378 us; the launch traced here: 377 us
  waiting for transfers between devices  131 us (35%)
  other arithmetic  88.7 us (23%)
  blocking collectives  57.2 us (15%)
  local copies, waits for them, and re-layouts  52.8 us (14%)
  between operations  17 us (4%)
  matrix products  16.4 us (4%)
  starting transfers between devices  13.6 us (4%)
    reduce_scatter x1, waiting for transfers between devices, on_device(): lax.psum_scatter(result.reshape(blocks * tokens, width_shard), 'tensor',...  82.4 us
    unnamed x4, other arithmetic  76.9 us
    psum x1, blocking collectives, on_device(): down_sum, up_sum = lax.psum((down_part, up_part), 'tensor')  38.9 us
    unnamed x25, local copies, waits for them, and re-layouts  26.8 us
    all_to_all x1, blocking collectives, on_device(): lax.all_to_all(change_up, ('tensor', 'dp'), split_axis=2, concat_axis=0,...  18.4 us
    all_to_all x1, waiting for transfers between devices, on_device(): lax.all_to_all(change_down, ('tensor', 'dp'), split_axis=2, concat_axis=0...  13.9 us
    all_to_all x1, waiting for transfers between devices, on_device(): lax.all_to_all(summed[0], 'tensor', split_axis=0, concat_axis=2, tiled=True)  13.9 us
    div x2, local copies, waits for them, and re-layouts, adam_step(): learn_rate * (moment_next / correct_one)  12.8 us
  transfers between devices with their start and end apart: 8, of which 6 were waited for; matrix products, arithmetic and copies ran while one was open for 21% of the time, Pallas kernels for 0%

commit v1 on v0

v1 whole, which is shorter than its diff:
```python
import functools

import jax
import jax.numpy as jnp
from jax import lax
from jax.experimental import pallas as pl
from jax.experimental.pallas import tpu as pltpu
from jax.sharding import PartitionSpec as P

MESH = pl.DeviceIdType.MESH

adapter_scale = 2.0
clip_norm = 12000.0
learn_rate = 0.004
beta_one = 0.9
beta_two = 0.999
adam_eps = 1e-08
correct_one = 1.0 - beta_one**20
correct_two = 1.0 - beta_two**20

EARLY_PAIR = 1
EARLY_LINE = 1


def adam_step(gradient, factor, moment, square):
    clipped = gradient * factor
    moment_next = beta_one * moment + (1.0 - beta_one) * clipped
    square_next = beta_two * square + (1.0 - beta_two) * clipped * clipped
    change = (
        learn_rate * (moment_next / correct_one) / (jnp.sqrt(square_next / correct_two) + adam_eps)
    )
    return (moment_next, square_next, change)


def line_order(line):
    order = []
    for near in range((line + 1) // 2):
        order.append(line - 1 - near)
        if near != line - 1 - near:
            order.append(near)
    return order


def kernel(
    n,
    owner_ref,
    tenant_ref,
    feat_ref,
    cot_ref,
    down_ref,
    up_ref,
    weight_ref,
    mom_down_ref,
    mom_up_ref,
    var_down_ref,
    var_up_ref,
    proj_ref,
    new_down_ref,
    new_up_ref,
    mean_down_ref,
    mean_up_ref,
    power_down_ref,
    power_up_ref,
    wbuf,
    state,
    rpart,
    rbuf,
    gsend,
    grecv,
    summed,
    owned,
    change,
    changes,
    ysend,
    yrecv,
    part,
    going_up,
    going_down,
    adapted,
    wsem,
    msem,
    rank_s,
    rank_r,
    g_s,
    g_r,
    a_s,
    a_r,
    c_s,
    c_r,
    f_s,
    f_r,
    y_s,
    y_r,
    z_s,
    u_r,
    d_r,
):
    tenants, lowrank, w = down_ref.shape
    tokens, depth = feat_ref.shape
    line = n // 2
    order = line_order(line)
    t = lax.axis_index("tensor")
    d = lax.axis_index("dp")
    zi, yi = t // 2, lax.rem(t, 2)
    mate = {"dp": 1 - d}
    pair = {"tensor": zi * 2 + 1 - yi}

    def peer(o):
        return lax.rem(t + o, n)

    def columns(block):
        return pl.ds(pl.multiple_of(block * w, w), w)

    barrier = pltpu.get_barrier_semaphore()

    @pl.loop(1, n)
    def _(o):
        pl.semaphore_signal(barrier, inc=1, device_id={"tensor": peer(o)}, device_id_type=MESH)

    pl.semaphore_signal(barrier, inc=1, device_id=mate, device_id_type=MESH)

    def weight_copy(i, block):
        return pltpu.make_async_copy(
            weight_ref.at[:, columns(block)], wbuf.at[i], wsem.at[i]
        )

    blocks = [z * 2 + 1 - yi for z in order] + [z * 2 + yi for z in order]
    for i, block in enumerate(blocks):
        weight_copy(i, block).start()
    state_copies = [
        pltpu.make_async_copy(ref, state.at[i], msem.at[i])
        for i, ref in enumerate((mom_down_ref, mom_up_ref, var_down_ref, var_up_ref))
    ]
    for copy in state_copies:
        copy.start()

    tenant = tenant_ref[...]
    contract = (((1,), (1,)), ((), ()))
    tenant_row = lax.broadcasted_iota(jnp.int32, (tenants, lowrank, tokens), 0)
    tenant_hit = tenant_row == tenant[None]

    def rank_part(adapter, rows):
        scores = lax.dot_general(
            adapter[...].reshape(tenants * lowrank, w),
            rows[...],
            contract,
            preferred_element_type=jnp.float32,
        ).reshape(tenants, lowrank, tokens)
        return jnp.sum(jnp.where(tenant_hit, scores, 0.0), axis=0)

    rpart[0] = rank_part(down_ref, feat_ref)
    rpart[1] = rank_part(up_ref, cot_ref)

    pl.semaphore_wait(barrier, n)

    def rank_copy(o, source):
        return pltpu.make_async_remote_copy(
            src_ref=rpart,
            dst_ref=rbuf.at[source],
            send_sem=rank_s.at[o],
            recv_sem=rank_r.at[source],
            device_id={"tensor": peer(o)},
            device_id_type=MESH,
        )

    @pl.loop(1, n)
    def _(o):
        rank_copy(o, t).start()

    def pair_copy(z):
        return pltpu.make_async_remote_copy(
            src_ref=ysend.at[z],
            dst_ref=yrecv.at[z],
            send_sem=y_s.at[z],
            recv_sem=y_r.at[z],
            device_id=pair,
            device_id_type=MESH,
        )

    def frozen(i, block):
        weight_copy(i, block).wait()
        return jnp.dot(feat_ref[...], wbuf[i], preferred_element_type=jnp.float32)

    for i, z in enumerate(order):
        ysend[z] = frozen(i, blocks[i])
        if i < EARLY_PAIR:
            pair_copy(z).start()

    slot = jnp.zeros_like(tenant)
    slot = lax.fori_loop(
        0, tenants, lambda k, s: jnp.where(tenant == k, owner_ref[k], s), slot
    )

    @pl.loop(1, n)
    def _(o):
        rank_copy(o, peer(o)).wait_recv()

    rbuf[t] = rpart[...]
    total = rbuf[0]
    for source in range(1, n):
        total = total + rbuf[source]
    low = adapter_scale * total
    down_low = low[0].astype(jnp.bfloat16).astype(jnp.float32)
    up_low = low[1].astype(jnp.bfloat16).astype(jnp.float32)

    half_row = lax.broadcasted_iota(jnp.int32, (n, lowrank, tokens), 0) * 2

    def half_grads(side):
        hit = half_row + side == slot[None]

        def one(values, rows):
            spread = jnp.where(hit, values[None], 0.0).reshape(n * lowrank, tokens)
            return jnp.dot(
                spread.astype(jnp.bfloat16), rows[...], preferred_element_type=jnp.float32
            ).reshape(n, lowrank, w)

        return one(up_low, feat_ref), one(down_low, cot_ref)

    def mate_copy(i):
        return pltpu.make_async_remote_copy(
            src_ref=gsend.at[i],
            dst_ref=grecv.at[i],
            send_sem=g_s.at[i],
            recv_sem=g_r.at[i],
            device_id=mate,
            device_id_type=MESH,
        )

    theirs = half_grads(1 - d)
    for i in range(2):
        gsend[i] = theirs[i]
    for i in range(2):
        mate_copy(i).start()
    mine = half_grads(d)
    for i in range(2):
        summed[:, i] = mine[i]
    for i in range(2):
        mate_copy(i).wait_recv()
        summed[:, i] = summed[:, i] + grecv[i]

    def grad_copy(o, source):
        return pltpu.make_async_remote_copy(
            src_ref=summed.at[peer(o)],
            dst_ref=owned.at[source],
            send_sem=a_s.at[o],
            recv_sem=a_r.at[source],
            device_id={"tensor": peer(o)},
            device_id_type=MESH,
        )

    @pl.loop(1, n)
    def _(o):
        grad_copy(o, t).start()

    for z in order[EARLY_PAIR:]:
        pair_copy(z).start()

    owned[t] = summed[t]

    down_spread = jnp.where(tenant_hit, down_low[None], 0.0).reshape(tenants * lowrank, tokens)
    adapted[...] = jnp.dot(
        jnp.transpose(down_spread).astype(jnp.bfloat16),
        up_ref[...].reshape(tenants * lowrank, w),
        preferred_element_type=jnp.float32,
    )
    for i, z in enumerate(order):
        part[z] = frozen(line + i, blocks[line + i])

    def up_copy(z):
        return pltpu.make_async_remote_copy(
            src_ref=part.at[z],
            dst_ref=going_up.at[z],
            send_sem=z_s.at[z],
            recv_sem=u_r.at[z],
            device_id={"tensor": lax.rem(t + 2, n)},
            device_id_type=MESH,
        )

    def down_copy(z):
        return pltpu.make_async_remote_copy(
            src_ref=part.at[z],
            dst_ref=going_down.at[z],
            send_sem=z_s.at[z],
            recv_sem=d_r.at[z],
            device_id={"tensor": lax.rem(t + n - 2, n)},
            device_id_type=MESH,
        )

    def pair_sum(z):
        pair_copy(z).wait_recv()
        part[z] = part[z] + yrecv[z]

    def ends(z):
        @pl.when(jnp.logical_and(zi == 0, z > 0))
        def _():
            up_copy(z).start()

        @pl.when(jnp.logical_and(zi == line - 1, z < line - 1))
        def _():
            down_copy(z).start()

    def middles(z):
        @pl.when(jnp.logical_and(zi > 0, zi < z))
        def _():
            up_copy(z).wait_recv()
            part[z] = part[z] + going_up[z]
            up_copy(z).start()

        @pl.when(jnp.logical_and(zi > z, zi < line - 1))
        def _():
            down_copy(z).wait_recv()
            part[z] = part[z] + going_down[z]
            down_copy(z).start()

    for z in order[:EARLY_LINE]:
        pair_sum(z)
        ends(z)

    for copy in state_copies:
        copy.wait()

    @pl.loop(1, n)
    def _(o):
        grad_copy(o, peer(o)).wait_recv()

    def squares_of(k, acc):
        g = owned[k]
        return acc + jnp.sum(g * g, axis=0)

    squares = lax.fori_loop(0, n, squares_of, jnp.zeros((lowrank, w), jnp.float32))
    squares = jnp.sum(squares, axis=(0, 1), keepdims=True)
    factor = clip_norm / jnp.maximum(jnp.sqrt(squares), clip_norm)

    def change_copy(o, source):
        return pltpu.make_async_remote_copy(
            src_ref=change.at[peer(o)],
            dst_ref=changes.at[source * 2 + d],
            send_sem=c_s.at[o],
            recv_sem=c_r.at[source],
            device_id={"tensor": peer(o)},
            device_id_type=MESH,
        )

    def step_piece(k):
        at = columns(k)
        for i, (mean_ref, power_ref) in enumerate(
            ((mean_down_ref, power_down_ref), (mean_up_ref, power_up_ref))
        ):
            mean, power, moved = adam_step(
                owned[k, i], factor, state[i, 0, :, at], state[2 + i, 0, :, at]
            )
            mean_ref[0, :, at] = mean
            power_ref[0, :, at] = power
            change[k, i] = moved

    @pl.loop(1, n)
    def _(o):
        step_piece(peer(o))

        @pl.when(o > 1)
        def _():
            change_copy(o - 1, t).start()

    step_piece(t)
    change_copy(n - 1, t).start()
    changes[t * 2 + d] = change[t]

    for z in order[EARLY_LINE:]:
        pair_sum(z)
        ends(z)

    def forward_copy(source, side):
        at = source * 2 + side
        return pltpu.make_async_remote_copy(
            src_ref=changes.at[at],
            dst_ref=changes.at[at],
            send_sem=f_s.at[source],
            recv_sem=f_r.at[source],
            device_id=mate,
            device_id_type=MESH,
        )

    forward_copy(t, d).start()
    for z in order:
        middles(z)

    @pl.loop(1, n)
    def _(o):
        change_copy(o, peer(n - o)).wait_recv()
        forward_copy(peer(n - o), d).start()

    @pl.when(zi > 0)
    def _():
        up_copy(zi).wait_recv()
        part[zi] = part[zi] + going_up[zi]

    @pl.when(zi < line - 1)
    def _():
        down_copy(zi).wait_recv()
        part[zi] = part[zi] + going_down[zi]

    proj_ref[...] = (part[zi] + adapted[...]).astype(proj_ref.dtype)

    @pl.loop(0, n)
    def _(source):
        forward_copy(source, 1 - d).wait_recv()

    @pl.loop(0, tenants)
    def _(k):
        back = changes[owner_ref[k]]
        new_down_ref[k] = (down_ref[k].astype(jnp.float32) - back[0]).astype(jnp.bfloat16)
        new_up_ref[k] = (up_ref[k].astype(jnp.float32) - back[1]).astype(jnp.bfloat16)

    @pl.loop(1, n)
    def _(o):
        rank_copy(o, t).wait_send()
        grad_copy(o, t).wait_send()
        change_copy(o, t).wait_send()

    @pl.loop(0, n)
    def _(source):
        forward_copy(source, d).wait_send()

    for i in range(2):
        mate_copy(i).wait_send()
    for z in order:
        pair_copy(z).wait_send()

        @pl.when(zi != z)
        def _():
            up_copy(z).wait_send()


def on_device(n, *args):
    (
        features,
        cotangent,
        token_tenant,
        owner_device,
        frozen_weight,
        adapter_down,
        adapter_up,
        momentum_down,
        momentum_up,
        variance_down,
        variance_up,
    ) = args
    tokens, depth = features.shape
    tenants, lowrank, w = adapter_down.shape
    line = n // 2
    f32 = jnp.float32
    vmem = pl.BlockSpec(memory_space=pltpu.VMEM)
    hbm = pl.BlockSpec(memory_space=pl.ANY)
    dma = pltpu.SemaphoreType.DMA
    shape = jax.ShapeDtypeStruct
    return pl.pallas_call(
        functools.partial(kernel, n),
        out_shape=(
            shape((tokens, w), jnp.bfloat16),
            shape(adapter_down.shape, jnp.bfloat16),
            shape(adapter_up.shape, jnp.bfloat16),
            shape(momentum_down.shape, f32),
            shape(momentum_up.shape, f32),
            shape(variance_down.shape, f32),
            shape(variance_up.shape, f32),
        ),
        in_specs=[pl.BlockSpec(memory_space=pltpu.SMEM)] + [vmem] * 5 + [hbm] * 5,
        out_specs=[vmem] * 7,
        scratch_shapes=[
            pltpu.VMEM((n, depth, w), jnp.bfloat16),
            pltpu.VMEM((4,) + momentum_down.shape, f32),
            pltpu.VMEM((2, lowrank, tokens), f32),
            pltpu.VMEM((n, 2, lowrank, tokens), f32),
            pltpu.VMEM((2, n, lowrank, w), f32),
            pltpu.VMEM((2, n, lowrank, w), f32),
            pltpu.VMEM((n, 2, lowrank, w), f32),
            pltpu.VMEM((n, 2, lowrank, w), f32),
            pltpu.VMEM((n, 2, lowrank, w), f32),
            pltpu.VMEM((tenants, 2, lowrank, w), f32),
            pltpu.VMEM((line, tokens, w), f32),
            pltpu.VMEM((line, tokens, w), f32),
            pltpu.VMEM((line, tokens, w), f32),
            pltpu.VMEM((line, tokens, w), f32),
            pltpu.VMEM((line, tokens, w), f32),
            pltpu.VMEM((tokens, w), f32),
            dma((n,)),
            dma((4,)),
            dma((n,)),
            dma((n,)),
            dma((2,)),
            dma((2,)),
            dma((n,)),
            dma((n,)),
            dma((n,)),
            dma((n,)),
            dma((n,)),
            dma((n,)),
            dma((line,)),
            dma((line,)),
            dma((line,)),
            dma((line,)),
            dma((line,)),
        ],
        compiler_params=pltpu.CompilerParams(
            collective_id=0, has_side_effects=True, vmem_limit_bytes=60 * 1024 * 1024
        ),
    )(
        owner_device,
        token_tenant.reshape(1, tokens),
        features,
        cotangent,
        adapter_down,
        adapter_up,
        frozen_weight,
        momentum_down,
        momentum_up,
        variance_down,
        variance_up,
    )


def solution(mesh):
    in_specs = (
        P(("group", "dp"), "tensor"),
        P(("group", "dp"), "tensor"),
        P(("group", "dp")),
        P("group"),
        P("tensor", None),
        P("group", None, "tensor"),
        P("group", None, "tensor"),
        P(("group", "tensor", "dp"), None, None),
        P(("group", "tensor", "dp"), None, None),
        P(("group", "tensor", "dp"), None, None),
        P(("group", "tensor", "dp"), None, None),
    )
    out_specs = (
        P(("group", "dp"), "tensor"),
        P("group", None, "tensor"),
        P("group", None, "tensor"),
        P(("group", "tensor", "dp"), None, None),
        P(("group", "tensor", "dp"), None, None),
        P(("group", "tensor", "dp"), None, None),
        P(("group", "tensor", "dp"), None, None),
    )
    return jax.shard_map(
        functools.partial(on_device, mesh.shape["tensor"]),
        mesh=mesh,
        in_specs=in_specs,
        out_specs=out_specs,
        check_vma=False,
    )
```

time: 378 us -> 127 us (0.34)
  waiting for transfers between devices: 131 us -> 0 us
  Pallas kernels: 0 us -> 113 us
  other arithmetic: 88.7 us -> 0 us
  blocking collectives: 57.2 us -> 0 us
  local copies, waits for them, and re-layouts: 52.8 us -> 12.9 us
  matrix products: 16.4 us -> 0 us
  between operations: 17 us -> 0.65 us
  starting transfers between devices: 13.6 us -> 0 us
    pallas_call x0 -> x1, Pallas kernels: none -> 113 us  [on_device(): pl.pallas_call(functools.partial(kernel, n), out_shape=(shape((tokens, w)...]
    reduce_scatter x3 -> x0, waiting for transfers between devices: 93.4 us -> none  [the longest x1 82.4 us: on_device(): lax.psum_scatter(result.reshape(blocks * tokens, width_shard), 'tensor',...]
    unnamed x4 -> x0, other arithmetic: 76.9 us -> none
    psum x1 -> x0, blocking collectives: 38.9 us -> none  [on_device(): down_sum, up_sum = lax.psum((down_part, up_part), 'tensor')]
    all_to_all x3 -> x0, waiting for transfers between devices: 36.7 us -> none  [the longest x1 13.9 us: on_device(): lax.all_to_all(change_down, ('tensor', 'dp'), split_axis=2, concat_axis=0...]
    all_to_all x1 -> x0, blocking collectives: 18.4 us -> none  [on_device(): lax.all_to_all(change_up, ('tensor', 'dp'), split_axis=2, concat_axis=0,...]
    dot_general x8 -> x0, matrix products: 16.4 us -> none  [the longest x1 10.1 us: frozen_blocks(): jnp.einsum('ti,ibc->btc', features, columns, preferred_element_type=jnp.f...]
    unnamed x25 -> x7, local copies, waits for them, and re-layouts: 26.8 us -> 12.9 us
  transfers between devices with their start and end apart: 8 -> 0, of which waited for: 6 -> 0; matrix products, arithmetic and copies ran while one was open for 21% -> 0% of each run, Pallas kernels for 0% -> 0%
where the time goes in v1:
time: 127 us
  Pallas kernels  113 us (89%)
  local copies, waits for them, and re-layouts  12.9 us (10%)
    pallas_call x1, Pallas kernels, on_device(): pl.pallas_call(functools.partial(kernel, n), out_shape=(shape((tokens, w)...  113 us
    unnamed x7, local copies, waits for them, and re-layouts  12.9 us

profile of v1, /device:TPU:0, one launch (start us, length us, event | category | flops | bytes accessed | tf_op | source)
XLA Modules:
  0.0 126.6 jit_solution(6899902154490570942)
XLA Ops:
  0.6 113.1 %shard_map.162 = (bf16[128,1024]{1,0:T(8,128)(2,1)}, bf16[16,16,1024]{2,1,0:T(8,128)(2,1)}, bf16[16,16,1024]{2,1,0:T(8,128)(2,1)}, f32[1,16,8192]{2,1,0:T(8,128)...) custom-call(s32[16]{0:T(128)} %owner_ref.1, s32[1,128]{1,0:T(1,128)} %bitcast.1, ...), custom_call_target="tpu_custom_call" | custom-call | tf_op jit(solution)/shard_map/pallas_call | solution.py:456
  113.7 1.7 %copy.25 = bf16[128,1024]{1,0:T(8,128)(2,1)} copy(bf16[128,1024]{1,0:T(8,128)(2,1)} %get-tuple-element.14) | data formatting | bytes 524288
  115.4 1.9 %copy.26 = bf16[16,16,1024]{2,1,0:T(8,128)(2,1)} copy(bf16[16,16,1024]{2,1,0:T(8,128)(2,1)} %get-tuple-element.15) | data formatting | bytes 1048576
  117.3 1.9 %copy.27 = bf16[16,16,1024]{2,1,0:T(8,128)(2,1)} copy(bf16[16,16,1024]{2,1,0:T(8,128)(2,1)} %get-tuple-element.16) | data formatting | bytes 1048576
  119.2 1.9 %copy.28 = f32[1,16,8192]{2,1,0:T(8,128)} copy(f32[1,16,8192]{2,1,0:T(8,128)} %get-tuple-element.17) | data formatting | bytes 1048576
  121.0 1.9 %copy.29 = f32[1,16,8192]{2,1,0:T(8,128)} copy(f32[1,16,8192]{2,1,0:T(8,128)} %get-tuple-element.18) | data formatting | bytes 1048576
  122.9 1.9 %copy.30 = f32[1,16,8192]{2,1,0:T(8,128)} copy(f32[1,16,8192]{2,1,0:T(8,128)} %get-tuple-element.19) | data formatting | bytes 1048576
  124.8 1.9 %copy.31 = f32[1,16,8192]{2,1,0:T(8,128)} copy(f32[1,16,8192]{2,1,0:T(8,128)} %get-tuple-element.20) | data formatting | bytes 1048576

commit v2 on v1

--- a/solution.py
+++ b/solution.py
@@ -18,8 +18,7 @@
 correct_one = 1.0 - beta_one**20
 correct_two = 1.0 - beta_two**20
 
-EARLY_PAIR = 1
-EARLY_LINE = 1
+CHUNKS = 2
 
 
 def adam_step(gradient, factor, moment, square):
@@ -105,8 +104,21 @@
     mate = {"dp": 1 - d}
     pair = {"tensor": zi * 2 + 1 - yi}
 
+    quarter = max(1, line // 4)
+    waves = (
+        order[:quarter],
+        order[quarter : 2 * quarter],
+        order[2 * quarter : 3 * quarter],
+        order[3 * quarter :],
+    )
+    height = tokens // CHUNKS
+    paired = n & (n - 1) == 0
+
     def peer(o):
-        return lax.rem(t + o, n)
+        return t ^ (n - o) if paired else lax.rem(t + o, n)
+
+    def giver(o):
+        return t ^ (n - o) if paired else lax.rem(t + n - o, n)
 
     def columns(block):
         return pl.ds(pl.multiple_of(block * w, w), w)
@@ -167,15 +179,22 @@
     def _(o):
         rank_copy(o, t).start()
 
-    def pair_copy(z):
-        return pltpu.make_async_remote_copy(
-            src_ref=ysend.at[z],
-            dst_ref=yrecv.at[z],
-            send_sem=y_s.at[z],
-            recv_sem=y_r.at[z],
+    def rows_of(c):
+        return pl.ds(c * height, height)
+
+    def pair_copy(z, c):
+        return pltpu.make_async_remote_copy(
+            src_ref=ysend.at[z, rows_of(c)],
+            dst_ref=yrecv.at[z, rows_of(c)],
+            send_sem=y_s.at[z * CHUNKS + c],
+            recv_sem=y_r.at[z * CHUNKS + c],
             device_id=pair,
             device_id_type=MESH,
         )
+
+    def pair_start(z):
+        for c in range(CHUNKS):
+            pair_copy(z, c).start()
 
     def frozen(i, block):
         weight_copy(i, block).wait()
@@ -183,8 +202,8 @@
 
     for i, z in enumerate(order):
         ysend[z] = frozen(i, blocks[i])
-        if i < EARLY_PAIR:
-            pair_copy(z).start()
+        if z in waves[0]:
+            pair_start(z)
 
     slot = jnp.zeros_like(tenant)
     slot = lax.fori_loop(
@@ -193,7 +212,7 @@
 
     @pl.loop(1, n)
     def _(o):
-        rank_copy(o, peer(o)).wait_recv()
+        rank_copy(o, giver(o)).wait_recv()
 
     rbuf[t] = rpart[...]
     total = rbuf[0]
@@ -252,8 +271,8 @@
     def _(o):
         grad_copy(o, t).start()
 
-    for z in order[EARLY_PAIR:]:
-        pair_copy(z).start()
+    for z in waves[1]:
+        pair_start(z)
 
     owned[t] = summed[t]
 
@@ -266,54 +285,57 @@
     for i, z in enumerate(order):
         part[z] = frozen(line + i, blocks[line + i])
 
-    def up_copy(z):
-        return pltpu.make_async_remote_copy(
-            src_ref=part.at[z],
-            dst_ref=going_up.at[z],
-            send_sem=z_s.at[z],
-            recv_sem=u_r.at[z],
+    def up_copy(z, c):
+        return pltpu.make_async_remote_copy(
+            src_ref=part.at[z, rows_of(c)],
+            dst_ref=going_up.at[z, rows_of(c)],
+            send_sem=z_s.at[z * CHUNKS + c],
+            recv_sem=u_r.at[z * CHUNKS + c],
             device_id={"tensor": lax.rem(t + 2, n)},
             device_id_type=MESH,
         )
 
-    def down_copy(z):
-        return pltpu.make_async_remote_copy(
-            src_ref=part.at[z],
-            dst_ref=going_down.at[z],
-            send_sem=z_s.at[z],
-            recv_sem=d_r.at[z],
+    def down_copy(z, c):
+        return pltpu.make_async_remote_copy(
+            src_ref=part.at[z, rows_of(c)],
+            dst_ref=going_down.at[z, rows_of(c)],
+            send_sem=z_s.at[z * CHUNKS + c],
+            recv_sem=d_r.at[z * CHUNKS + c],
             device_id={"tensor": lax.rem(t + n - 2, n)},
             device_id_type=MESH,
         )
 
-    def pair_sum(z):
-        pair_copy(z).wait_recv()
-        part[z] = part[z] + yrecv[z]
-
     def ends(z):
-        @pl.when(jnp.logical_and(zi == 0, z > 0))
-        def _():
-            up_copy(z).start()
-
-        @pl.when(jnp.logical_and(zi == line - 1, z < line - 1))
-        def _():
-            down_copy(z).start()
+        for c in range(CHUNKS):
+            at = rows_of(c)
+            pair_copy(z, c).wait_recv()
+            part[z, at] = part[z, at] + yrecv[z, at]
+
+            @pl.when(jnp.logical_and(zi == 0, z > 0))
+            def _():
+                up_copy(z, c).start()
+
+            @pl.when(jnp.logical_and(zi == line - 1, z < line - 1))
+            def _():
+                down_copy(z, c).start()
 
     def middles(z):
-        @pl.when(jnp.logical_and(zi > 0, zi < z))
-        def _():
-            up_copy(z).wait_recv()
-            part[z] = part[z] + going_up[z]
-            up_copy(z).start()
-
-        @pl.when(jnp.logical_and(zi > z, zi < line - 1))
-        def _():
-            down_copy(z).wait_recv()
-            part[z] = part[z] + going_down[z]
-            down_copy(z).start()
-
-    for z in order[:EARLY_LINE]:
-        pair_sum(z)
+        for c in range(CHUNKS):
+            at = rows_of(c)
+
+            @pl.when(jnp.logical_and(zi > 0, zi < z))
+            def _():
+                up_copy(z, c).wait_recv()
+                part[z, at] = part[z, at] + going_up[z, at]
+                up_copy(z, c).start()
+
+            @pl.when(jnp.logical_and(zi > z, zi < line - 1))
+            def _():
+                down_copy(z, c).wait_recv()
+                part[z, at] = part[z, at] + going_down[z, at]
+                down_copy(z, c).start()
+
+    for z in waves[0]:
         ends(z)
 
     for copy in state_copies:
@@ -321,7 +343,10 @@
 
     @pl.loop(1, n)
     def _(o):
-        grad_copy(o, peer(o)).wait_recv()
+        grad_copy(o, giver(o)).wait_recv()
+
+    for z in waves[2]:
+        pair_start(z)
 
     def squares_of(k, acc):
         g = owned[k]
@@ -343,14 +368,12 @@
 
     def step_piece(k):
         at = columns(k)
-        for i, (mean_ref, power_ref) in enumerate(
-            ((mean_down_ref, power_down_ref), (mean_up_ref, power_up_ref))
-        ):
+        for i in range(2):
             mean, power, moved = adam_step(
                 owned[k, i], factor, state[i, 0, :, at], state[2 + i, 0, :, at]
             )
-            mean_ref[0, :, at] = mean
-            power_ref[0, :, at] = power
+            state[i, 0, :, at] = mean
+            state[2 + i, 0, :, at] = power
             change[k, i] = moved
 
     @pl.loop(1, n)
@@ -364,10 +387,6 @@
     step_piece(t)
     change_copy(n - 1, t).start()
     changes[t * 2 + d] = change[t]
-
-    for z in order[EARLY_LINE:]:
-        pair_sum(z)
-        ends(z)
 
     def forward_copy(source, side):
         at = source * 2 + side
@@ -381,25 +400,31 @@
         )
 
     forward_copy(t, d).start()
-    for z in order:
+    state_outs = [
+        pltpu.make_async_copy(state.at[i], ref, msem.at[i])
+        for i, ref in enumerate((mean_down_ref, mean_up_ref, power_down_ref, power_up_ref))
+    ]
+    for copy in state_outs:
+        copy.start()
+
+    for z in waves[3]:
+        pair_start(z)
+    for z in waves[1]:
+        ends(z)
+    for z in waves[0]:
         middles(z)
-
-    @pl.loop(1, n)
-    def _(o):
-        change_copy(o, peer(n - o)).wait_recv()
-        forward_copy(peer(n - o), d).start()
-
-    @pl.when(zi > 0)
-    def _():
-        up_copy(zi).wait_recv()
-        part[zi] = part[zi] + going_up[zi]
-
-    @pl.when(zi < line - 1)
-    def _():
-        down_copy(zi).wait_recv()
-        part[zi] = part[zi] + going_down[zi]
-
-    proj_ref[...] = (part[zi] + adapted[...]).astype(proj_ref.dtype)
+    for z in waves[2]:
+        ends(z)
+
+    @pl.loop(1, n)
+    def _(o):
+        change_copy(o, giver(o)).wait_recv()
+        forward_copy(giver(o), d).start()
+
+    for z in waves[3]:
+        ends(z)
+    for z in waves[1] + waves[2]:
+        middles(z)
 
     @pl.loop(0, n)
     def _(source):
@@ -411,6 +436,27 @@
         new_down_ref[k] = (down_ref[k].astype(jnp.float32) - back[0]).astype(jnp.bfloat16)
         new_up_ref[k] = (up_ref[k].astype(jnp.float32) - back[1]).astype(jnp.bfloat16)
 
+    for z in waves[3]:
+        middles(z)
+
+    for c in range(CHUNKS):
+        at = rows_of(c)
+
+        @pl.when(zi > 0)
+        def _():
+            up_copy(zi, c).wait_recv()
+            part[zi, at] = part[zi, at] + going_up[zi, at]
+
+        @pl.when(zi < line - 1)
+        def _():
+            down_copy(zi, c).wait_recv()
+            part[zi, at] = part[zi, at] + going_down[zi, at]
+
+        proj_ref[at] = (part[zi, at] + adapted[at]).astype(proj_ref.dtype)
+
+    for copy in state_outs:
+        copy.wait()
+
     @pl.loop(1, n)
     def _(o):
         rank_copy(o, t).wait_send()
@@ -424,11 +470,27 @@
     for i in range(2):
         mate_copy(i).wait_send()
     for z in order:
-        pair_copy(z).wait_send()
-
-        @pl.when(zi != z)
-        def _():
-            up_copy(z).wait_send()
+        for c in range(CHUNKS):
+            pair_copy(z, c).wait_send()
+
+            @pl.when(zi != z)
+            def _():
+                up_copy(z, c).wait_send()
+
+
+def hand_out(*refs):
+    count = len(refs) // 3
+    sources, results, held = refs[:count], refs[count : 2 * count], refs[2 * count : 3 * count]
+    sems = refs[-1]
+    ins = [pltpu.make_async_copy(sources[i], held[i], sems.at[0, i]) for i in range(count)]
+    outs = [pltpu.make_async_copy(held[i], results[i], sems.at[1, i]) for i in range(count)]
+    for copy in ins:
+        copy.start()
+    for i in range(count):
+        ins[i].wait()
+        outs[i].start()
+    for copy in outs:
+        copy.wait()
 
 
 def on_device(n, *args):
@@ -453,7 +515,7 @@
     hbm = pl.BlockSpec(memory_space=pl.ANY)
     dma = pltpu.SemaphoreType.DMA
     shape = jax.ShapeDtypeStruct
-    return pl.pallas_call(
+    results = pl.pallas_call(
         functools.partial(kernel, n),
         out_shape=(
             shape((tokens, w), jnp.bfloat16),
@@ -465,7 +527,7 @@
             shape(variance_up.shape, f32),
         ),
         in_specs=[pl.BlockSpec(memory_space=pltpu.SMEM)] + [vmem] * 5 + [hbm] * 5,
-        out_specs=[vmem] * 7,
+        out_specs=[vmem] * 3 + [hbm] * 4,
         scratch_shapes=[
             pltpu.VMEM((n, depth, w), jnp.bfloat16),
             pltpu.VMEM((4,) + momentum_down.shape, f32),
@@ -495,11 +557,11 @@
             dma((n,)),
             dma((n,)),
             dma((n,)),
-            dma((line,)),
-            dma((line,)),
-            dma((line,)),
-            dma((line,)),
-            dma((line,)),
+            dma((line * CHUNKS,)),
+            dma((line * CHUNKS,)),
+            dma((line * CHUNKS,)),
+            dma((line * CHUNKS,)),
+            dma((line * CHUNKS,)),
         ],
         compiler_params=pltpu.CompilerParams(
             collective_id=0, has_side_effects=True, vmem_limit_bytes=60 * 1024 * 1024
@@ -517,6 +579,14 @@
         variance_down,
         variance_up,
     )
+    return pl.pallas_call(
+        hand_out,
+        out_shape=tuple(shape(r.shape, r.dtype) for r in results),
+        in_specs=[hbm] * len(results),
+        out_specs=[hbm] * len(results),
+        scratch_shapes=[pltpu.VMEM(r.shape, r.dtype) for r in results]
+        + [dma((2, len(results)))],
+    )(*results)
 
 
 def solution(mesh):

time: 127 us -> 106 us (0.83)
  the two profiles are of different devices: /device:TPU:0 before, /device:TPU:16 now
where the time goes in v2:
time: 106 us
  Pallas kernels  105 us (99%)
    pallas_call x1, Pallas kernels, on_device(): pl.pallas_call(functools.partial(kernel, n), out_shape=(shape((tokens, w)...  102 us
    pallas_call x1, Pallas kernels, on_device(): pl.pallas_call(hand_out, out_shape=tuple((shape(r.shape, r.dtype) for r i...  2.93 us

profile of v2, /device:TPU:16, one launch (start us, length us, event | category | flops | bytes accessed | tf_op | source)
XLA Modules:
  0.0 105.7 jit_solution(6545079835095044865)
XLA Ops:
  0.6 102.1 %shard_map.162 = (bf16[128,1024]{1,0:T(8,128)(2,1)}, bf16[16,16,1024]{2,1,0:T(8,128)(2,1)}, bf16[16,16,1024]{2,1,0:T(8,128)(2,1)}, f32[1,16,8192]{2,1,0:T(8,128)...) custom-call(s32[16]{0:T(128)} %owner_ref.1, s32[1,128]{1,0:T(1,128)} %bitcast.1, ...), custom_call_target="tpu_custom_call" | custom-call | tf_op jit(solution)/shard_map/pallas_call | solution.py:518
  102.7 2.9 %shard_map.163 = (bf16[128,1024]{1,0:T(8,128)(2,1)}, bf16[16,16,1024]{2,1,0:T(8,128)(2,1)}, bf16[16,16,1024]{2,1,0:T(8,128)(2,1)}, f32[1,16,8192]{2,1,0:T(8,128)...) custom-call(bf16[128,1024]{1,0:T(8,128)(2,1)} %get-tuple-element.14.refs_0_, ...), custom_call_target="tpu_custom_call" | custom-call | tf_op jit(solution)/shard_map/pallas_call | solution.py:582
